TPU v7x, 128 devices: a whole 4x4x4 slice. The times are simulated.
128 devices in a mesh: section: 8 (over y, core), fsdp: 16 (over x, z).
Axes of the slice: x: 4, y: 4, z: 4, core: 2. Of those that a mesh axis runs over, the one named last changes fastest.
Arguments:
- layer_input: bfloat16 [8, 8192, 2048], P('section', 'fsdp'), may hold values from -6 to 6
- resid_grad: bfloat16 [8, 8192, 2048], P('section', 'fsdp'), may hold values from -6 to 6
- qkv_grad: bfloat16 [8, 8192, 3072], P('section', 'fsdp'), may hold values from -6 to 6
- prev_input: bfloat16 [8, 8192, 2048], P('section', 'fsdp'), may hold values from -6 to 6
- prev_qkv_grad: bfloat16 [8, 8192, 3072], P('section', 'fsdp'), may hold values from -0.059814453 to 0.059814453
- qkv_weight: bfloat16 [8, 2048, 3072], P('section', 'fsdp'), may hold values from -0.125 to 0.125
- norm_gain: float32 [8, 2048], P('section'), may hold values from 0.1 to 1.9
Outputs:
- upstream_grad: bfloat16 [8, 8192, 2048], P('section', 'fsdp')
- weight_grad: float32 [8, 2048, 3072], P('section', 'fsdp')
- gain_grad: float32 [8, 2048], P('section')
All inputs are finite; a program needn't handle non-finite values.
Results may differ from a plain program's by a relative error of at most 0.018.
Values may be sent and summed in bfloat16 or wider, within the bound.
A program may use at most 128 MiB of HBM per device.

v0:
```python
import jax
import jax.numpy as jnp
from jax import lax
from jax.sharding import PartitionSpec as P

EPS = 1e-05


def from_behind(block, axis, distance):
    devices = range(lax.axis_size(axis))
    route = [(i - distance, i) for i in devices if i - distance in devices]
    return lax.ppermute(block, axis, route)


def row_scale(rows):
    values = rows.astype(jnp.float32)
    return lax.rsqrt(jnp.mean(values * values, axis=-1, keepdims=True) + EPS)


def transpose_product(grads, piece):
    return lax.dot_general(
        grads, piece, (((1,), (1,)), ((), ())), preferred_element_type=jnp.float32
    )


def local(layer_input, resid_grad, qkv_grad, prev_input, prev_qkv_grad, qkv_weight, norm_gain):
    rows_now = layer_input[0]
    grads_now = qkv_grad[0]
    rows_prev = prev_input[0]
    grads_prev = prev_qkv_grad[0]
    weight_rows = qkv_weight[0]
    gain = norm_gain[0]
    owned = weight_rows.shape[0]
    prev_scale = row_scale(rows_prev)
    prev_normed = (rows_prev.astype(jnp.float32) * prev_scale * gain[None, :]).astype(jnp.bfloat16)
    direction = transpose_product(
        grads_now, lax.all_gather(weight_rows, "fsdp", axis=0, tiled=True)
    )
    scale = row_scale(rows_now)
    values = rows_now.astype(jnp.float32)
    gained = gain[None, :] * direction
    inner = jnp.mean(gained * values, axis=-1, keepdims=True)
    local_grad = (
        resid_grad[0].astype(jnp.float32) + scale * gained - values * scale * scale * scale * inner
    ).astype(jnp.bfloat16)
    upstream_grad = from_behind(local_grad, "section", -1)
    upstream_grad, ready_rows = lax.optimization_barrier((upstream_grad, prev_normed))
    weight_grad = lax.psum_scatter(
        lax.dot_general(
            ready_rows, grads_prev, (((0,), (0,)), ((), ())), preferred_element_type=jnp.float32
        ).astype(jnp.bfloat16),
        "fsdp",
        scatter_dimension=0,
        tiled=True,
    ).astype(jnp.float32)
    owned_gain = lax.dynamic_slice_in_dim(gain, lax.axis_index("fsdp") * owned, owned, 0)
    gain_part = jnp.sum(weight_rows.astype(jnp.float32) * weight_grad, axis=1) / owned_gain
    gain_grad = lax.all_gather(gain_part, "fsdp", axis=0, tiled=True)
    return (upstream_grad[None], weight_grad[None], gain_grad[None])


def solution(mesh):
    placed = (
        P("section", "fsdp", None),
        P("section", "fsdp", None),
        P("section", "fsdp", None),
        P("section", "fsdp", None),
        P("section", "fsdp", None),
        P("section", "fsdp", None),
        P("section", None),
    )
    return jax.shard_map(
        local,
        mesh=mesh,
        in_specs=placed,
        out_specs=(P("section", "fsdp", None), P("section", "fsdp", None), P("section", None)),
        check_vma=False,
    )
```

profile of v0, /device:TPU:1, one launch (start us, length us, event | category | flops | bytes accessed | tf_op | source)
XLA Modules:
  0.0 283.6 jit_solution(17675918492956940125)
XLA Ops:
  7.2 0.0 copy-start
  7.2 0.0 all-gather.4.cloned.1.call-start
  7.2 0.7 all-gather.4.cloned.1.call-update
  7.9 0.0 reduce-scatter.2.cloned.1.call-start
  8.0 2.2 fusion.2
  10.2 93.4 %all-gather.4.cloned.1.call-done = bf16[1,2048,3072]{2,1,0:T(8,128)(2,1)} async-done(((bf16[1,128,3072]{2,1,0:T(8,128)(2,1)}), bf16[1,2048,3072]{2,1,0:T(8,128)(2,1)}) %all-gather.4.cloned.1.call-update) | async-done | bytes 12582928 | tf_op jit(solution)/shard_map/all_gather | solution.py:37
  103.6 0.0 copy-start.1
  103.6 15.5 %fusion.5 = (f32[512]{0:T(512)S(1)}, f32[512]{0:T(512)S(1)}, bf16[512,2048]{1,0:T(8,128)(2,1)}, f32[512,2048]{1,0:T(8,128)}) fusion(bf16[1,512,2048]{2,1,0:T(8,128)(2,1)} %param.7, f32[2048]{0:T(1024)} %bitcast.41, f32[512]{0:T(512)S(1)} %add_rsqrt_fusion, bf16[1,512,2048]{2,1,0:T(8,128)(2,1)} %param.10, ...), kind=kOutput, calls=%fused_computation.11 | convolution fusion | flops 6452935680 | bytes 26228736 | tf_op jit(solution)/shard_map/dot_general | solution.py:21
  119.1 0.0 copy-done.1
  119.1 0.0 copy-start.2
  119.1 5.3 %fusion.10 = bf16[512,2048]{1,0:T(8,128)(2,1)S(1)} fusion(f32[512,2048]{1,0:T(8,128)} %get-tuple-element.10, bf16[1,512,2048]{2,1,0:T(8,128)(2,1)} %param.8, bf16[1,512,2048]{2,1,0:T(8,128)(2,1)} %param.7, f32[512]{0:T(512)S(1)} %get-tuple-element.12, f32[2048]{0:T(1024)S(1)} %bitcast.42, f32[512]{0:T(512)S(1)} %get-tuple-element.11), kind=kLoop, calls=%fused_computation.16 | loop fusion | flops 11534336 | bytes 10498048 | tf_op jit(solution)/shard_map/convert_element_type | solution.py:45
  124.4 2.6 collective-permute-start
  127.0 24.9 %collective-permute-done = bf16[512,2048]{1,0:T(8,128)(2,1)} collective-permute-done((bf16[512,2048]{1,0:T(8,128)(2,1)S(1)}, bf16[512,2048]{1,0:T(8,128)(2,1)}, u32[]{:S(2)}, u32[]{:S(2)}) %collective-permute-start) | collective-permute-done | bytes 2097184 | tf_op jit(solution)/shard_map/ppermute | solution.py:12
  151.9 0.0 copy-done
  151.9 0.0 copy-done.2
  151.9 9.7 %convolution_convert_fusion = bf16[2048,3072]{1,0:T(8,128)(2,1)} fusion(bf16[512,2048]{1,0:T(8,128)(2,1)S(1)} %copy-done.2, bf16[1,512,3072]{2,1,0:T(8,128)(2,1)S(1)} %copy-done), kind=kOutput, calls=%fused_computation.2 | convolution fusion | flops 6448742400 | bytes 17825792 | tf_op jit(solution)/shard_map/dot_general | solution.py:49
  161.6 0.0 reduce-scatter.2.cloned.1.call-update
  161.6 93.4 %reduce-scatter.2.cloned.1.call-done = bf16[128,3072]{1,0:T(8,128)(2,1)} async-done(((bf16[2048,3072]{1,0:T(8,128)(2,1)}), bf16[128,3072]{1,0:T(8,128)(2,1)}) %reduce-scatter.2.cloned.1.call-update) | async-done | bytes 786448 | tf_op jit(solution)/shard_map/reduce_scatter | solution.py:48
  255.0 1.7 fusion.14
  256.7 13.9 %all-gather.1 = f32[16,1,128]{2,1,0:T(1,128)S(1)} all-gather(f32[1,1,128]{2,1,0:T(1,128)S(1)} %fusion.15), channel_id=1, replica_groups=mesh['section'=8,'fsdp'=16] {'fsdp'}, dimensions={0}, use_global_device_ids=true | all-gather | bytes 8704 | tf_op jit(solution)/shard_map/all_gather | solution.py:58
  270.6 2.4 convert_bitcast_fusion
  273.0 3.2 %copy.12 = bf16[1,512,2048]{2,1,0:T(8,128)(2,1)} copy(bf16[1,512,2048]{2,1,0:T(8,128)(2,1)} %bitcast.8) | data formatting | bytes 4194304
  276.1 0.6 copy.13
  (3 shorter events, 0.0 us)
Async XLA Ops:
  7.2 144.7 %copy-start = (bf16[1,512,3072]{2,1,0:T(8,128)(2,1)S(1)}, bf16[1,512,3072]{2,1,0:T(8,128)(2,1)}, u32[]{:S(2)}) copy-start(bf16[1,512,3072]{2,1,0:T(8,128)(2,1)} %param.11) | copy-start | bytes 9437188
  7.2 96.4 %all-gather.4.cloned.1.call-start = ((), (), s32[]{:S(2)}) async-start(), calls=%async_computation.2 | async-start | bytes 13369344 | tf_op jit(solution)/shard_map/all_gather | solution.py:37
  7.9 247.1 %reduce-scatter.2.cloned.1.call-start = ((), (), s32[]{:S(2)}) async-start(), calls=%async_computation.1 | async-start | bytes 13369344 | tf_op jit(solution)/shard_map/reduce_scatter | solution.py:48
  103.6 15.5 %copy-start.1 = (f32[1,2048]{1,0:T(1,128)S(1)}, f32[1,2048]{1,0:T(1,128)}, u32[]{:S(2)}) copy-start(f32[1,2048]{1,0:T(1,128)} %param.13) | copy-start | bytes 24580
  119.1 32.8 %copy-start.2 = (bf16[512,2048]{1,0:T(8,128)(2,1)S(1)}, bf16[512,2048]{1,0:T(8,128)(2,1)}, u32[]{:S(2)}) copy-start(bf16[512,2048]{1,0:T(8,128)(2,1)} %get-tuple-element.6) | copy-start | bytes 6291460
  124.4 27.5 %collective-permute-start = (bf16[512,2048]{1,0:T(8,128)(2,1)S(1)}, bf16[512,2048]{1,0:T(8,128)(2,1)}, u32[]{:S(2)}, u32[]{:S(2)}) collective-permute-start(bf16[512,2048]{1,0:T(8,128)(2,1)S(1)} %fusion.10), channel_id=1, source_target_pairs={{16,0},{32,16},{48,32},{64,48},{80,64},{96,80},{112,96},{17,1},{33... | collective-permute-start | bytes 6291464 | tf_op jit(solution)/shard_map/ppermute | solution.py:12
Sparse Core Ops, SparseCore 0:
  10.2 93.3 all-gather.3
  161.7 93.2 reduce-scatter.1
where the time goes:
time: 289 us; the launch traced here: 284 us
  waiting for transfers between devices  212 us (73%)
  matrix products  25.2 us (9%)
  between operations  14.1 us (5%)
  blocking collectives  13.9 us (5%)
  other arithmetic  11.6 us (4%)
  local copies, waits for them, and re-layouts  3.78 us (1%)
    all_gather x1, waiting for transfers between devices, local(): lax.all_gather(weight_rows, 'fsdp', axis=0, tiled=True)  93.4 us
    reduce_scatter x1, waiting for transfers between devices, local(): lax.psum_scatter(lax.dot_general(ready_rows, grads_prev, (((0,), (0,)), (...  93.4 us
    ppermute x1, waiting for transfers between devices, from_behind(): return lax.ppermute(block, axis, route)  24.9 us
    dot_general x1, matrix products, transpose_product(): lax.dot_general(grads, piece, (((1,), (1,)), ((), ())), preferred_element...  15.5 us
    all_gather x1, blocking collectives, local(): gain_grad = lax.all_gather(gain_part, 'fsdp', axis=0, tiled=True)  13.9 us
    dot_general x1, matrix products, local(): lax.dot_general(ready_rows, grads_prev, (((0,), (0,)), ((), ())), preferr...  9.72 us
  transfers between devices with their start and end apart: 3, of which 3 were waited for; matrix products, arithmetic and copies ran while one was open for 1% of the time, Pallas kernels for 0%

commit v1 on v0

--- a/solution.py
+++ b/solution.py
@@ -44,10 +44,9 @@
         resid_grad[0].astype(jnp.float32) + scale * gained - values * scale * scale * scale * inner
     ).astype(jnp.bfloat16)
     upstream_grad = from_behind(local_grad, "section", -1)
-    upstream_grad, ready_rows = lax.optimization_barrier((upstream_grad, prev_normed))
     weight_grad = lax.psum_scatter(
         lax.dot_general(
-            ready_rows, grads_prev, (((0,), (0,)), ((), ())), preferred_element_type=jnp.float32
+            prev_normed, grads_prev, (((0,), (0,)), ((), ())), preferred_element_type=jnp.float32
         ).astype(jnp.bfloat16),
         "fsdp",
         scatter_dimension=0,

time: 289 us -> 235 us (0.81)
  the two profiles are of different devices: /device:TPU:1 before, /device:TPU:0 now
where the time goes in v1:
time: 235 us
  waiting for transfers between devices  164 us (70%)
  matrix products  22.9 us (10%)
  blocking collectives  19.3 us (8%)
  between operations  14.1 us (6%)
  other arithmetic  9.45 us (4%)
  local copies, waits for them, and re-layouts  3.78 us (2%)
    reduce_scatter x1, waiting for transfers between devices, local(): lax.psum_scatter(lax.dot_general(prev_normed, grads_prev, (((0,), (0,)),...  82.1 us
    all_gather x1, waiting for transfers between devices, local(): lax.all_gather(weight_rows, 'fsdp', axis=0, tiled=True)  81 us
    all_gather x1, blocking collectives, local(): gain_grad = lax.all_gather(gain_part, 'fsdp', axis=0, tiled=True)  19.3 us
    dot_general x1, matrix products, local(): lax.dot_general(prev_normed, grads_prev, (((0,), (0,)), ((), ())), prefer...  11.6 us
    dot_general x1, matrix products, transpose_product(): lax.dot_general(grads, piece, (((1,), (1,)), ((), ())), preferred_element...  11.3 us
  transfers between devices with their start and end apart: 3, of which 2 were waited for; matrix products, arithmetic and copies ran while one was open for 14% of the time, Pallas kernels for 0%

profile of v1, /device:TPU:0, one launch (start us, length us, event | category | flops | bytes accessed | tf_op | source)
XLA Modules:
  0.0 234.6 jit_solution(13687583729323604503)
XLA Ops:
  7.2 0.0 copy-start
  7.2 0.0 all-gather.4.cloned.1.call-start
  7.2 0.7 all-gather.4.cloned.1.call-update
  7.9 0.0 reduce-scatter.2.cloned.1.call-start
  8.0 2.2 fusion.2
  10.2 0.0 copy-done
  10.2 11.6 %convolution_convert_fusion = bf16[2048,3072]{1,0:T(8,128)(2,1)} fusion(bf16[1,512,3072]{2,1,0:T(8,128)(2,1)S(1)} %copy-done, bf16[1,512,2048]{2,1,0:T(8,128)(2,1)} %param.10, f32[2048]{0:T(1024)} %bitcast.39, f32[512]{0:T(512)S(1)} %add_rsqrt_fusion), kind=kOutput, calls=%fused_computation.2 | convolution fusion | flops 6452936704 | bytes 17836032 | tf_op jit(solution)/shard_map/dot_general | solution.py:48
  21.8 0.0 copy-start.3
  21.8 0.0 reduce-scatter.2.cloned.1.call-update
  21.8 81.0 %all-gather.4.cloned.1.call-done = bf16[1,2048,3072]{2,1,0:T(8,128)(2,1)} async-done(((bf16[1,128,3072]{2,1,0:T(8,128)(2,1)}), bf16[1,2048,3072]{2,1,0:T(8,128)(2,1)}) %all-gather.4.cloned.1.call-update) | async-done | bytes 12582928 | tf_op jit(solution)/shard_map/all_gather | solution.py:37
  102.8 0.0 copy-done.3
  102.8 0.0 copy-start.1
  102.8 0.0 copy-start.2
  102.9 11.3 %fusion.5 = (f32[512]{0:T(512)S(1)}, f32[512]{0:T(512)S(1)}, f32[512,2048]{1,0:T(8,128)S(1)}) fusion(bf16[1,512,2048]{2,1,0:T(8,128)(2,1)} %param.7, f32[2048]{0:T(1024)S(1)} %bitcast.40, bf16[1,2048,3072]{2,1,0:T(8,128)(2,1)} %all-gather.4.cloned.1.call-done, bf16[1,512,3072]{2,1,0:T(8,128)(2,1)} %param.9), kind=kOutput, calls=%fused_computation.11 | convolution fusion | flops 6448741376 | bytes 22032384 | tf_op jit(solution)/shard_map/dot_general | solution.py:21
  114.2 0.0 copy-done.1
  114.2 0.0 copy-done.2
  114.2 3.1 %fusion.10 = bf16[512,2048]{1,0:T(8,128)(2,1)} fusion(f32[512,2048]{1,0:T(8,128)S(1)} %get-tuple-element.5, bf16[1,512,2048]{2,1,0:T(8,128)(2,1)S(1)} %copy-done.2, bf16[1,512,2048]{2,1,0:T(8,128)(2,1)S(1)} %copy-done.1, f32[512]{0:T(512)S(1)} %get-tuple-element.7, f32[2048]{0:T(1024)S(1)} %bitcast.41, f32[512]{0:T(512)S(1)} %get-tuple-element.6), kind=kLoop, calls=%fused_computation.16 | loop fusion | flops 11534336 | bytes 10498048 | tf_op jit(solution)/shard_map/convert_element_type | solution.py:45
  117.3 1.3 collective-permute-start
  118.6 82.1 %reduce-scatter.2.cloned.1.call-done = bf16[128,3072]{1,0:T(8,128)(2,1)} async-done(((bf16[2048,3072]{1,0:T(8,128)(2,1)}), bf16[128,3072]{1,0:T(8,128)(2,1)}) %reduce-scatter.2.cloned.1.call-update) | async-done | bytes 786448 | tf_op jit(solution)/shard_map/reduce_scatter | solution.py:47
  200.6 1.7 fusion.18
  202.3 19.3 %all-gather.1 = f32[16,1,128]{2,1,0:T(1,128)S(1)} all-gather(f32[1,1,128]{2,1,0:T(1,128)S(1)} %fusion.19), channel_id=1, replica_groups=mesh['section'=8,'fsdp'=16] {'fsdp'}, dimensions={0}, use_global_device_ids=true | all-gather | bytes 8704 | tf_op jit(solution)/shard_map/all_gather | solution.py:57
  221.6 2.4 %convert_bitcast_fusion = f32[1,128,3072]{2,1,0:T(8,128)} fusion(bf16[128,3072]{1,0:T(8,128)(2,1)} %reduce-scatter.2.cloned.1.call-done), kind=kLoop, calls=%fused_computation.25 | loop fusion | flops 393216 | bytes 2359296 | tf_op jit(solution)/shard_map/broadcast_in_dim | solution.py:58
  224.0 0.0 collective-permute-done
  224.0 3.2 %copy.12 = bf16[1,512,2048]{2,1,0:T(8,128)(2,1)} copy(bf16[1,512,2048]{2,1,0:T(8,128)(2,1)} %bitcast.6) | data formatting | bytes 4194304
  227.2 0.6 copy.13
  (3 shorter events, 0.0 us)
Async XLA Ops:
  7.2 3.0 %copy-start = (bf16[1,512,3072]{2,1,0:T(8,128)(2,1)S(1)}, bf16[1,512,3072]{2,1,0:T(8,128)(2,1)}, u32[]{:S(2)}) copy-start(bf16[1,512,3072]{2,1,0:T(8,128)(2,1)} %param.11) | copy-start | bytes 9437188
  7.2 95.7 %all-gather.4.cloned.1.call-start = ((), (), s32[]{:S(2)}) async-start(), calls=%async_computation.2 | async-start | bytes 13369344 | tf_op jit(solution)/shard_map/all_gather | solution.py:37
  7.9 192.7 %reduce-scatter.2.cloned.1.call-start = ((), (), s32[]{:S(2)}) async-start(), calls=%async_computation.1 | async-start | bytes 13369344 | tf_op jit(solution)/shard_map/reduce_scatter | solution.py:47
  21.8 81.1 %copy-start.3 = (f32[1,2048]{1,0:T(1,128)S(1)}, f32[1,2048]{1,0:T(1,128)}, u32[]{:S(2)}) copy-start(f32[1,2048]{1,0:T(1,128)} %param.13) | copy-start | bytes 24580
  102.8 11.3 %copy-start.1 = (bf16[1,512,2048]{2,1,0:T(8,128)(2,1)S(1)}, bf16[1,512,2048]{2,1,0:T(8,128)(2,1)}, u32[]{:S(2)}) copy-start(bf16[1,512,2048]{2,1,0:T(8,128)(2,1)} %param.7) | copy-start | bytes 6291460
  102.8 11.3 %copy-start.2 = (bf16[1,512,2048]{2,1,0:T(8,128)(2,1)S(1)}, bf16[1,512,2048]{2,1,0:T(8,128)(2,1)}, u32[]{:S(2)}) copy-start(bf16[1,512,2048]{2,1,0:T(8,128)(2,1)} %param.8) | copy-start | bytes 6291460
  117.3 106.7 %collective-permute-start = (bf16[512,2048]{1,0:T(8,128)(2,1)}, bf16[512,2048]{1,0:T(8,128)(2,1)}, u32[]{:S(2)}, u32[]{:S(2)}) collective-permute-start(bf16[512,2048]{1,0:T(8,128)(2,1)} %fusion.10), channel_id=1, source_target_pairs={{16,0},{32,16},{48,32},{64,48},{80,64},{96,80},{112,96},{17,1},{33... | collective-permute-start | bytes 6291464 | tf_op jit(solution)/shard_map/ppermute | solution.py:12
Sparse Core Ops, SparseCore 0:
  10.2 92.5 all-gather.3
  106.3 94.3 reduce-scatter.1

commit v2 on v1

v2 whole, which is shorter than its diff:
```python
import functools

import jax
import jax.numpy as jnp
from jax import lax
from jax.experimental import pallas as pl
from jax.experimental.pallas import tpu as pltpu
from jax.sharding import PartitionSpec as P

EPS = 1e-05
MESH = pl.DeviceIdType.MESH
TOK, D, QKV = 512, 2048, 3072
HALF = TOK // 2
OWN = 128
PIECE = 64
F32, BF16 = jnp.float32, jnp.bfloat16


def kernel(
    x_hbm, res_hbm, q_hbm, prev_hbm, g_hbm, w_hbm, gain_ref,
    up_hbm, wg_hbm, gg_ref,
    w_full, dw, r1, r2, r3, r4, wout, w_own, q_work, normed, n_sib, g_work, g_sib, dirs, x_buf, res_buf, gain_row,
    load_sem, w_sem, ws_sem, tn_sem, tg_sem, tq_sem, sn_sem, sg_sem, rd_sem, r1_sem, r2_sem, r3_sem, r4_sem, lg_sem, gg_sem,
    send_sem, gsend_sem,
):
    s, f = lax.axis_index("section"), lax.axis_index("fsdp")
    c, x, z = s % 2, f // 4, f % 4
    away = (c + x) % 2
    is_away, is_home, has_before = away == 1, away == 0, s > 0

    def at(section, x_to, z_to):
        return (section, ((x_to + 4) % 4) * 4 + (z_to + 4) % 4)

    sib_section = s + 1 - 2 * c
    sibling, across = at(sib_section, x, z), at(s, x + 2, z)
    up, down = at(s, x, z + 1), at(s, x, z - 1)
    left, right = at(sib_section, x - 1, z), at(sib_section, x + 1, z)
    before, after = ((s + 7) % 8, f), ((s + 1) % 8, f)

    sent = []

    def send(make, when=None):
        n = len(sent)

        def build():
            src, dst, recv, device = make()
            return pltpu.make_async_remote_copy(
                src_ref=src, dst_ref=dst, send_sem=send_sem.at[n], recv_sem=recv, device_id=device, device_id_type=MESH
            )

        sent.append([build, when])
        build().start()
        return n

    def wait_sent(n):
        build, when = sent[n]
        if build is None:
            return
        sent[n][0] = None
        if when is None:
            build().wait_send()
        else:
            pl.when(when)(lambda: build().wait_send())

    def load(src, dst, sem):
        copy = pltpu.make_async_copy(src, dst, sem)
        copy.start()
        return copy

    def arrive(dst, sem):
        pltpu.make_async_copy(dst, dst, sem).wait()

    barrier = pltpu.get_barrier_semaphore()

    def greet(device):
        pl.semaphore_signal(barrier, inc=1, device_id=device, device_id_type=MESH)

    @pl.loop(1, 16)
    def _(j):
        greet((s, (f + j) % 16))

    greet(sibling)

    @pl.when(is_away)
    def _():
        greet(left)
        greet(right)

    goes_down = (c == 0) & (s > 0)
    comes_down = (c == 1) & (s < 7)

    @pl.when(goes_down)
    def _():
        greet(before)

    @pl.when(comes_down)
    def _():
        greet(after)

    prev_load = load(prev_hbm, x_buf, load_sem.at[0])
    own_load = load(w_hbm, w_own, load_sem.at[1])
    res_load = load(res_hbm, res_buf, load_sem.at[2])

    pl.semaphore_wait(barrier, 16 + 2 * away + (goes_down | comes_down).astype(jnp.int32))

    def w_piece(k, dz, h, flip=0):
        kind = away if flip == 0 else 1 - away
        xv = x + 2 * k
        owner = (xv + 3 * kind) % 4 if h == 0 else (xv + kind) % 4
        inner = PIECE * kind if h == 0 else PIECE * (1 - kind)
        start = (4 * owner + (z + dz + 4) % 4) * OWN + inner
        return w_full.at[pl.ds(pl.multiple_of(start, PIECE), PIECE)]

    def w_flag(k, dz, h):
        return w_sem.at[8 * ((dz + 4) % 4) + 2 * k + h]

    def ws_flag(k, dz, h):
        return ws_sem.at[8 * ((dz + 4) % 4) + 2 * k + h]

    def to_sibling(k, dz, h):
        send(lambda: (w_piece(k, dz, h), w_piece(k, dz, h), ws_flag(k, dz, h), sibling))

    def to_z(k, dz, h, way):
        send(lambda: (w_piece(k, dz, h), w_piece(k, dz, h), w_flag(k, dz - way, h), up if way == 1 else down))

    def to_column(h):
        send(lambda: (w_piece(0, 0, h), w_piece(0, 0, h), w_flag(1, 0, h), across))

    def spread_own():
        for h in range(2):
            to_column(h)
            to_z(0, 0, h, 1)
            to_z(0, 0, h, -1)
            to_sibling(0, 0, h)

    @pl.when(is_home)
    def _():
        for h in range(2):
            load(w_hbm.at[pl.ds(PIECE * h, PIECE)], w_piece(0, 0, h), w_flag(0, 0, h))
            rows = pl.ds(HALF * h, HALF)
            load(g_hbm.at[rows], g_work.at[rows], tg_sem.at[h])
            load(q_hbm.at[rows], q_work.at[rows], tq_sem.at[h])

    own_rows = pl.multiple_of(f * OWN, OWN)

    @pl.when(is_away)
    def _():
        for h in range(2):

            def own_piece(h=h):
                rows = w_full.at[pl.ds(pl.multiple_of(own_rows + PIECE * h, PIECE), PIECE)]
                return w_hbm.at[pl.ds(PIECE * h, PIECE)], rows, w_flag(0, 0, 1 - h), right if h == 1 else left

            send(own_piece, is_away)

    prev_load.wait()

    @pl.loop(0, TOK // 16)
    def _(i):
        rows = pl.ds(pl.multiple_of(i * 16, 16), 16)
        values = x_buf[rows, :].astype(F32)
        scale = lax.rsqrt(jnp.mean(values * values, axis=-1, keepdims=True) + EPS)
        normed[away, rows, :] = (values * scale * gain_ref[...]).astype(BF16)

    for h in range(2):
        arrive(w_piece(0, 0, h), w_flag(0, 0, h))
    spread_own()
    x_load = load(x_hbm, x_buf, load_sem.at[0])

    def trade(src, dst, sems, h):
        mine, theirs = pl.ds(HALF * h, HALF), pl.ds(HALF * (1 - h), HALF)
        return send(lambda: (src().at[mine], dst().at[theirs], sems(1 - h), left if h == 0 else right), is_away)

    tokens = []

    @pl.when(is_away)
    def _():
        for h in range(2):
            tokens.append(trade(lambda: normed.at[1], lambda: normed.at[0], lambda i: tn_sem.at[i], h))
            tokens.append(trade(lambda: g_hbm, lambda: g_work, lambda i: tg_sem.at[i], h))

    def blocks_of(kind):
        xa = (x + kind) % 4
        return xa, (xa + 2) % 4

    def tokens_to_sibling():
        for j, xb in enumerate(blocks_of(1 - away)):

            def features(j=j, xb=xb):
                columns = pl.ds(pl.multiple_of(512 * xb, 512), 512)
                return normed.at[0, :, columns], n_sib.at[:, pl.ds(512 * j, 512)], sn_sem.at[j], sibling

            send(features)
        send(lambda: (g_work, g_sib, sg_sem, sibling))

    @pl.when(is_home)
    def _():
        for h in range(2):
            arrive(g_work.at[pl.ds(HALF * h, HALF)], tg_sem.at[h])

    for h in range(2):
        arrive(w_piece(1, 0, h), w_flag(1, 0, h))
        to_z(1, 0, h, 1)
        to_z(1, 0, h, -1)
        to_sibling(1, 0, h)
    for k in range(2):
        for h in range(2):
            arrive(w_piece(k, -1, h), w_flag(k, -1, h))
            if h == 0:
                to_z(k, -1, 0, 1)
            arrive(w_piece(k, 1, h), w_flag(k, 1, h))
            if h == 1:
                to_z(k, 1, 1, -1)
            to_sibling(k, -1, h)
            to_sibling(k, 1, h)

    @pl.when(is_away)
    def _():
        for h in range(2):
            arrive(normed.at[0, pl.ds(HALF * h, HALF)], tn_sem.at[h])
            arrive(g_work.at[pl.ds(HALF * h, HALF)], tg_sem.at[h])

    tokens_to_sibling()

    @pl.when(is_away)
    def _():
        for n in tokens:
            wait_sent(n)
        for h in range(2):
            trade(lambda: q_hbm, lambda: q_work, lambda i: tq_sem.at[i], h)

    for j in range(2):
        arrive(n_sib.at[:, pl.ds(512 * j, 512)], sn_sem.at[j])
    arrive(g_sib, sg_sem)
    xa, xb = blocks_of(away)

    def product(dz):
        to = (z + dz) % 4

        def columns(ref, block):
            return ref[:, pl.ds(pl.multiple_of(512 * block + OWN * to, OWN), OWN)]

        mine = jnp.concatenate([columns(normed.at[0], xa), columns(normed.at[0], xb)], axis=1)
        theirs = jnp.concatenate([columns(n_sib, 0), columns(n_sib, 1)], axis=1)

        @pl.loop(0, 4)
        def _(j):
            span = pl.ds(pl.multiple_of(j * 768, 768), 768)
            dims = (((0,), (0,)), ((), ()))
            total = lax.dot_general(mine, g_work[:, span], dims, preferred_element_type=F32)
            total += lax.dot_general(theirs, g_sib[:, span], dims, preferred_element_type=F32)
            dw[dz, :, span] = total.astype(BF16)

    def d_piece(dz, k, h):
        at_home = 128 * k + 64 * h
        at_away = 128 * k if h == 1 else 192 - 128 * k
        return dw.at[dz, pl.ds(pl.multiple_of(at_home + away * (at_away - at_home), PIECE), PIECE)]

    product(2)
    first = []
    for k in (1, 0):
        first.append(send(lambda k=k: (d_piece(2, k, 0), r1.at[0, k], r1_sem.at[k], up)))
        first.append(send(lambda k=k: (d_piece(2, k, 1), r1.at[1, k], r1_sem.at[2 + k], down)))
    product(1)
    product(3)
    product(0)

    for k in range(2):
        for h in range(2):
            arrive(w_piece(k, 2, h), w_flag(k, 2, h))
            to_sibling(k, 2, h)

    def to_next(k, h, way):
        dz, side = (1, 0) if way == 1 else (3, 1)
        send(lambda: (d_piece(dz, k, h), r2.at[side, k, h], r2_sem.at[4 * side + 2 * k + h], up if way == 1 else down))

    for n in first[:2]:
        wait_sent(n)
    for k in (1, 0):
        to_next(k, 1, 1)
        to_next(k, 0, -1)

    for h in range(2):
        arrive(q_work.at[pl.ds(HALF * h, HALF)], tq_sem.at[h])
    for dz in range(4):
        for k in range(2):
            for h in range(2):
                arrive(w_piece(k, dz, h, 1), ws_flag(k, dz, h))

    for block in range(4):

        @pl.loop(0, 2)
        def _(j):
            rows = pl.ds(pl.multiple_of(512 * block + 256 * j, 256), 256)
            out = lax.dot_general(q_work[...], w_full[rows, :], (((1,), (1,)), ((), ())), preferred_element_type=F32)
            dirs[0, :, rows] = out.astype(BF16)

        @pl.when(is_away)
        def _():
            columns = pl.ds(512 * block, 512)
            for h in range(2):
                flags = functools.partial(lambda block, i: rd_sem.at[i, block], block)
                trade(lambda: dirs.at[0, :, columns], lambda: dirs.at[1, :, columns], flags, h)

    def add_into(target, term):
        @pl.loop(0, QKV // 512)
        def _(j):
            span = pl.ds(pl.multiple_of(j * 512, 512), 512)
            target[:, span] = (target[:, span].astype(F32) + term[:, span].astype(F32)).astype(BF16)

    for k in (1, 0):
        arrive(r1.at[0, k], r1_sem.at[k])
        add_into(d_piece(1, k, 0), r1.at[0, k])
        to_next(k, 0, 1)
        arrive(r1.at[1, k], r1_sem.at[2 + k])
        add_into(d_piece(3, k, 1), r1.at[1, k])
        to_next(k, 1, -1)

    @pl.when(is_away)
    def _():
        for h in range(2):
            for block in range(4):
                arrive(dirs.at[1, pl.ds(HALF * h, HALF), pl.ds(512 * block, 512)], rd_sem.at[h, block])

    x_load.wait()
    res_load.wait()
    for part in range(4):

        @pl.loop(0, 8)
        def _(i):
            rows = pl.ds(pl.multiple_of(128 * part + i * 16, 16), 16)
            values = x_buf[rows, :].astype(F32)
            scale = lax.rsqrt(jnp.mean(values * values, axis=-1, keepdims=True) + EPS)
            gained = gain_ref[...] * dirs[away, rows, :].astype(F32)
            inner = jnp.mean(gained * values, axis=-1, keepdims=True)
            out = res_buf[rows, :].astype(F32) + scale * gained - values * (scale * scale * scale * inner)
            res_buf[rows, :] = out.astype(BF16)

        @pl.when(has_before)
        def _():
            rows = pl.ds(128 * part, 128)
            send(lambda part=part: (res_buf.at[rows], up_hbm.at[rows], lg_sem.at[part], before), has_before)

    def sum_into(target, k, h):
        @pl.loop(0, QKV // 512)
        def _(j):
            span = pl.ds(pl.multiple_of(j * 512, 512), 512)
            total = target[:, span].astype(F32) + r2[0, k, h, :, span].astype(F32) + r2[1, k, h, :, span].astype(F32)
            target[:, span] = total.astype(BF16)

    def r2_arrive(k, h):
        arrive(r2.at[0, k, h], r2_sem.at[2 * k + h])
        arrive(r2.at[1, k, h], r2_sem.at[4 + 2 * k + h])

    for h in range(2):
        r2_arrive(1, h)
        sum_into(d_piece(0, 1, h), 1, h)
        send(lambda h=h: (d_piece(0, 1, h), r3.at[h], r3_sem.at[h], across))

    own_load.wait()
    for h in range(2):
        r2_arrive(0, h)
        arrive(r3.at[h], r3_sem.at[h])
        target = d_piece(0, 0, h)

        @pl.loop(0, QKV // 512)
        def _(j):
            span = pl.ds(pl.multiple_of(j * 512, 512), 512)
            total = target[:, span].astype(F32) + r2[0, 0, h, :, span].astype(F32) + r2[1, 0, h, :, span].astype(F32)
            total += r3[h, :, span].astype(F32)
            wout[pl.ds(PIECE * h, PIECE), span] = total
            target[:, span] = total.astype(BF16)

        @pl.when(is_away)
        def _():
            send(lambda h=h: (d_piece(0, 0, h), r4.at[1 - h], r4_sem.at[1 - h], left if h == 0 else right), is_away)

    @pl.when(is_away)
    def _():
        for h in range(2):
            arrive(r4.at[h], r4_sem.at[h])

            @pl.loop(0, QKV // 512)
            def _(j):
                span = pl.ds(pl.multiple_of(j * 512, 512), 512)
                wout[pl.ds(PIECE * h, PIECE), span] = r4[h, :, span].astype(F32)

    w_store = load(wout, wg_hbm, load_sem.at[3])

    def fold(i, total):
        span = pl.ds(pl.multiple_of(i * 128, 128), 128)
        return total + w_own[:, span].astype(F32) * wout[:, span]

    folded = lax.fori_loop(0, QKV // 128, fold, jnp.zeros((OWN, 128), F32))
    part = jnp.sum(folded.T, axis=0, keepdims=True) / gain_ref[:, pl.ds(own_rows, OWN)]
    gain_row[...] = part
    gg_ref[f, :, :] = part

    def gain_copy(j, source):
        return pltpu.make_async_remote_copy(
            src_ref=gain_row, dst_ref=gg_ref.at[source], send_sem=gsend_sem.at[j], recv_sem=gg_sem.at[source],
            device_id=(s, (f + j) % 16), device_id_type=MESH,
        )

    @pl.loop(1, 16)
    def _(j):
        gain_copy(j, f).start()

    @pl.when(s < 7)
    def _():
        for part in range(4):
            rows = pl.ds(128 * part, 128)
            arrive(up_hbm.at[rows], lg_sem.at[part])

    @pl.loop(1, 16)
    def _(j):
        source = (f + 16 - j) % 16
        gain_copy(j, source).wait_recv()
        gain_copy(j, f).wait_send()

    w_store.wait()
    for n in range(len(sent)):
        wait_sent(n)


SENDS = 120


def local(layer_input, resid_grad, qkv_grad, prev_input, prev_qkv_grad, qkv_weight, norm_gain):
    hbm = pl.BlockSpec(memory_space=pl.ANY)
    vmem = pl.BlockSpec(memory_space=pltpu.VMEM)
    dma = pltpu.SemaphoreType.DMA
    received, weight_grad, gain_rows = pl.pallas_call(
        kernel,
        out_shape=(
            jax.ShapeDtypeStruct((TOK, D), BF16),
            jax.ShapeDtypeStruct((OWN, QKV), F32),
            jax.ShapeDtypeStruct((16, 1, OWN), F32),
        ),
        in_specs=[hbm] * 6 + [vmem],
        out_specs=(hbm, hbm, vmem),
        scratch_shapes=[
            pltpu.VMEM((D, QKV), BF16),
            pltpu.VMEM((4, 256, QKV), BF16),
            pltpu.VMEM((2, 2, PIECE, QKV), BF16),
            pltpu.VMEM((2, 2, 2, PIECE, QKV), BF16),
            pltpu.VMEM((2, PIECE, QKV), BF16),
            pltpu.VMEM((2, PIECE, QKV), BF16),
            pltpu.VMEM((OWN, QKV), F32),
            pltpu.VMEM((OWN, QKV), BF16),
            pltpu.VMEM((TOK, QKV), BF16),
            pltpu.VMEM((2, TOK, D), BF16),
            pltpu.VMEM((TOK, D // 2), BF16),
            pltpu.VMEM((TOK, QKV), BF16),
            pltpu.VMEM((TOK, QKV), BF16),
            pltpu.VMEM((2, TOK, D), BF16),
            pltpu.VMEM((TOK, D), BF16),
            pltpu.VMEM((TOK, D), BF16),
            pltpu.VMEM((1, OWN), F32),
            dma((4,)),
            dma((32,)),
            dma((32,)),
            dma((2,)),
            dma((2,)),
            dma((2,)),
            dma((2,)),
            dma(()),
            dma((2, 4)),
            dma((4,)),
            dma((8,)),
            dma((2,)),
            dma((2,)),
            dma((4,)),
            dma((16,)),
            dma((SENDS,)),
            dma((16,)),
        ],
        compiler_params=pltpu.CompilerParams(collective_id=0, has_side_effects=True, vmem_limit_bytes=62 << 20),
    )(layer_input[0], resid_grad[0], qkv_grad[0], prev_input[0], prev_qkv_grad[0], qkv_weight[0], norm_gain)
    last = lax.axis_index("section") == lax.axis_size("section") - 1
    upstream_grad = jnp.where(last, jnp.zeros_like(received), received)
    return (upstream_grad[None], weight_grad[None], gain_rows.reshape(1, D))


def solution(mesh):
    tokens, whole = P("section", "fsdp", None), P("section", None)
    return jax.shard_map(
        local,
        mesh=mesh,
        in_specs=(tokens,) * 6 + (whole,),
        out_specs=(tokens, tokens, whole),
        check_vma=False,
    )
```

time: 235 us -> 153 us (0.65)
  the two profiles are of different devices: /device:TPU:0 before, /device:TPU:1 now
where the time goes in v2:
time: 153 us; the launch traced here: 151 us
  Pallas kernels  145 us (95%)
  other arithmetic  3.17 us (2%)
  local copies, waits for them, and re-layouts  1.75 us (1%)
    pallas_call x1, Pallas kernels, local(): pl.pallas_call(kernel, out_shape=(jax.ShapeDtypeStruct((TOK, D), BF16), j...  145 us
    broadcast_in_dim x1, other arithmetic, local(): return (upstream_grad[None], weight_grad[None], gain_rows.reshape(1, D))  3.17 us

profile of v2, /device:TPU:1, one launch (start us, length us, event | category | flops | bytes accessed | tf_op | source)
XLA Modules:
  0.0 151.0 jit_solution(12688337385378915981)
XLA Ops:
  0.6 145.4 %shard_map.94 = (bf16[512,2048]{1,0:T(8,128)(2,1)}, f32[128,3072]{1,0:T(8,128)}, f32[16,1,128]{2,1,0:T(1,128)}) custom-call(bf16[512,2048]{1,0:T(8,128)(2,1)} %bitcast.12, bf16[512,2048]{1,0:T(8,128)(2,1)} %bitcast.13, bf16[512,3072]{1,0:T(8,128)(2,1)} %bitcast.10, bf16[512,2048]{1,0:T(8,128)(2,1)} %bitcast.14, bf16[512,3072]{1,0:T(8,128)(2,1)} %bitcast.11, ...), custom_call_target="tpu_custom_call" | custom-call | tf_op jit(solution)/shard_map/pallas_call | solution.py:433
  146.0 0.0 copy-start
  146.1 3.2 %select_bitcast_fusion = bf16[1,512,2048]{2,1,0:T(8,128)(2,1)} fusion(bf16[512,2048]{1,0:T(8,128)(2,1)} %get-tuple-element.6, pred[]{:T(512)S(6)} %eq.3), kind=kLoop, calls=%fused_computation | loop fusion | flops 1048576 | bytes 4194305 | tf_op jit(solution)/shard_map/broadcast_in_dim | solution.py:482
  149.2 0.0 copy-start.1
  149.2 0.0 copy-done
  149.2 1.1 copy.12
  150.4 0.0 copy-done.1
  150.4 0.6 copy.13
Async XLA Ops:
  146.0 3.2 %copy-start = (f32[128,3072]{1,0:T(8,128)S(1)}, f32[128,3072]{1,0:T(8,128)}, u32[]{:S(2)}) copy-start(f32[128,3072]{1,0:T(8,128)} %get-tuple-element.7) | copy-start | bytes 4718596
  149.2 1.1 copy-start.1

commit v3 on v2

--- a/solution.py
+++ b/solution.py
@@ -11,6 +11,7 @@
 MESH = pl.DeviceIdType.MESH
 TOK, D, QKV = 512, 2048, 3072
 HALF = TOK // 2
+CHUNK = HALF // 2
 OWN = 128
 PIECE = 64
 F32, BF16 = jnp.float32, jnp.bfloat16
@@ -19,8 +20,8 @@
 def kernel(
     x_hbm, res_hbm, q_hbm, prev_hbm, g_hbm, w_hbm, gain_ref,
     up_hbm, wg_hbm, gg_ref,
-    w_full, dw, r1, r2, r3, r4, wout, w_own, q_work, normed, n_sib, g_work, g_sib, dirs, x_buf, res_buf, gain_row,
-    load_sem, w_sem, ws_sem, tn_sem, tg_sem, tq_sem, sn_sem, sg_sem, rd_sem, r1_sem, r2_sem, r3_sem, r4_sem, lg_sem, gg_sem,
+    w_full, dw, r1, r2, r3, r4, wout, q_work, normed, n_sib, g_work, g_sib, dirs, x_buf, res_buf, gain_part, gain_sib, gain_all,
+    load_sem, w_sem, ws_sem, tn_sem, tg_sem, tq_sem, sn_sem, sg_sem, rd_sem, r1_sem, r2_sem, r3_sem, r4_sem, lg_sem, gp_sem, gg_sem,
     send_sem, gsend_sem,
 ):
     s, f = lax.axis_index("section"), lax.axis_index("fsdp")
@@ -97,10 +98,6 @@
     def _():
         greet(after)
 
-    prev_load = load(prev_hbm, x_buf, load_sem.at[0])
-    own_load = load(w_hbm, w_own, load_sem.at[1])
-    res_load = load(res_hbm, res_buf, load_sem.at[2])
-
     pl.semaphore_wait(barrier, 16 + 2 * away + (goes_down | comes_down).astype(jnp.int32))
 
     def w_piece(k, dz, h, flip=0):
@@ -123,23 +120,25 @@
     def to_z(k, dz, h, way):
         send(lambda: (w_piece(k, dz, h), w_piece(k, dz, h), w_flag(k, dz - way, h), up if way == 1 else down))
 
-    def to_column(h):
-        send(lambda: (w_piece(0, 0, h), w_piece(0, 0, h), w_flag(1, 0, h), across))
-
-    def spread_own():
-        for h in range(2):
-            to_column(h)
-            to_z(0, 0, h, 1)
-            to_z(0, 0, h, -1)
-            to_sibling(0, 0, h)
+    def own_across(source, when):
+        for h in range(2):
+            send(lambda h=h: (source(h), w_piece(0, 0, h), w_flag(1, 0, h), across), when)
+
+    def spread_own(source, when):
+        for h in range(2):
+            send(lambda h=h: (source(h), w_piece(0, 0, h), w_flag(0, -1, h), up), when)
+            send(lambda h=h: (source(h), w_piece(0, 0, h), w_flag(0, 1, h), down), when)
+        for h in range(2):
+            send(lambda h=h: (source(h), w_piece(0, 0, h), ws_flag(0, 0, h), sibling), when)
+
+    def half_rows(h):
+        return w_hbm.at[pl.ds(PIECE * h, PIECE)]
 
     @pl.when(is_home)
     def _():
-        for h in range(2):
-            load(w_hbm.at[pl.ds(PIECE * h, PIECE)], w_piece(0, 0, h), w_flag(0, 0, h))
-            rows = pl.ds(HALF * h, HALF)
-            load(g_hbm.at[rows], g_work.at[rows], tg_sem.at[h])
-            load(q_hbm.at[rows], q_work.at[rows], tq_sem.at[h])
+        spread_own(half_rows, is_home)
+        for h in range(2):
+            load(half_rows(h), w_piece(0, 0, h), w_flag(0, 0, h))
 
     own_rows = pl.multiple_of(f * OWN, OWN)
 
@@ -149,9 +148,36 @@
 
             def own_piece(h=h):
                 rows = w_full.at[pl.ds(pl.multiple_of(own_rows + PIECE * h, PIECE), PIECE)]
-                return w_hbm.at[pl.ds(PIECE * h, PIECE)], rows, w_flag(0, 0, 1 - h), right if h == 1 else left
+                return half_rows(h), rows, w_flag(0, 0, 1 - h), right if h == 1 else left
 
             send(own_piece, is_away)
+
+    prev_load = load(prev_hbm, x_buf, load_sem.at[0])
+    res_load = load(res_hbm, res_buf, load_sem.at[2])
+
+    def chunk(h, i):
+        return pl.ds(HALF * h + CHUNK * i, CHUNK)
+
+    def whole(h):
+        return pl.ds(HALF * h, HALF)
+
+    def trade(src, dst, flag, h, rows=whole):
+        send(lambda: (src().at[rows(h)], dst().at[rows(1 - h)], flag(1 - h), left if h == 0 else right), is_away)
+
+    def trade_g(i):
+        for h in range(2):
+            trade(lambda: g_hbm, lambda: g_work, lambda h: tg_sem.at[h, i], h, lambda h: chunk(h, i))
+
+    def g_to_sibling(source, i, when):
+        for h in range(2):
+            send(lambda h=h: (source.at[chunk(h, i)], g_sib.at[chunk(h, i)], sg_sem.at[h, i], sibling), when)
+
+    @pl.when(is_home)
+    def _():
+        for h in range(2):
+            for i in range(2):
+                load(g_hbm.at[chunk(h, i)], g_work.at[chunk(h, i)], tg_sem.at[h, i])
+            load(q_hbm.at[whole(h)], q_work.at[whole(h)], tq_sem.at[h])
 
     prev_load.wait()
 
@@ -162,48 +188,51 @@
         scale = lax.rsqrt(jnp.mean(values * values, axis=-1, keepdims=True) + EPS)
         normed[away, rows, :] = (values * scale * gain_ref[...]).astype(BF16)
 
-    for h in range(2):
-        arrive(w_piece(0, 0, h), w_flag(0, 0, h))
-    spread_own()
-    x_load = load(x_hbm, x_buf, load_sem.at[0])
-
-    def trade(src, dst, sems, h):
-        mine, theirs = pl.ds(HALF * h, HALF), pl.ds(HALF * (1 - h), HALF)
-        return send(lambda: (src().at[mine], dst().at[theirs], sems(1 - h), left if h == 0 else right), is_away)
-
-    tokens = []
-
-    @pl.when(is_away)
-    def _():
-        for h in range(2):
-            tokens.append(trade(lambda: normed.at[1], lambda: normed.at[0], lambda i: tn_sem.at[i], h))
-            tokens.append(trade(lambda: g_hbm, lambda: g_work, lambda i: tg_sem.at[i], h))
-
     def blocks_of(kind):
         xa = (x + kind) % 4
         return xa, (xa + 2) % 4
 
-    def tokens_to_sibling():
-        for j, xb in enumerate(blocks_of(1 - away)):
-
-            def features(j=j, xb=xb):
-                columns = pl.ds(pl.multiple_of(512 * xb, 512), 512)
+    sib_blocks = blocks_of(1 - away)
+
+    def n_to_sibling(when):
+        for j, block in enumerate(sib_blocks):
+
+            def features(j=j, block=block):
+                columns = pl.ds(pl.multiple_of(512 * block, 512), 512)
                 return normed.at[0, :, columns], n_sib.at[:, pl.ds(512 * j, 512)], sn_sem.at[j], sibling
 
-            send(features)
-        send(lambda: (g_work, g_sib, sg_sem, sibling))
+            send(features, when)
+
+    for h in range(2):
+        arrive(w_piece(0, 0, h), w_flag(0, 0, h))
+
+    @pl.when(is_away)
+    def _():
+        own_across(lambda h: w_piece(0, 0, h), is_away)
+        spread_own(lambda h: w_piece(0, 0, h), is_away)
+        for h in range(2):
+            trade(lambda: normed.at[1], lambda: normed.at[0], lambda h: tn_sem.at[h], h)
 
     @pl.when(is_home)
     def _():
-        for h in range(2):
-            arrive(g_work.at[pl.ds(HALF * h, HALF)], tg_sem.at[h])
+        own_across(half_rows, is_home)
+        n_to_sibling(is_home)
+        for i in range(2):
+            g_to_sibling(g_hbm, i, is_home)
+
+    x_load = load(x_hbm, x_buf, load_sem.at[0])
 
     for h in range(2):
         arrive(w_piece(1, 0, h), w_flag(1, 0, h))
         to_z(1, 0, h, 1)
         to_z(1, 0, h, -1)
         to_sibling(1, 0, h)
-    for k in range(2):
+
+    @pl.when(is_away)
+    def _():
+        trade_g(0)
+
+    def pass_on(k):
         for h in range(2):
             arrive(w_piece(k, -1, h), w_flag(k, -1, h))
             if h == 0:
@@ -214,24 +243,38 @@
             to_sibling(k, -1, h)
             to_sibling(k, 1, h)
 
-    @pl.when(is_away)
-    def _():
-        for h in range(2):
-            arrive(normed.at[0, pl.ds(HALF * h, HALF)], tn_sem.at[h])
-            arrive(g_work.at[pl.ds(HALF * h, HALF)], tg_sem.at[h])
-
-    tokens_to_sibling()
-
-    @pl.when(is_away)
-    def _():
-        for n in tokens:
-            wait_sent(n)
-        for h in range(2):
-            trade(lambda: q_hbm, lambda: q_work, lambda i: tq_sem.at[i], h)
+    pass_on(0)
+
+    @pl.when(is_away)
+    def _():
+        trade_g(1)
+        for h in range(2):
+            arrive(normed.at[0, whole(h)], tn_sem.at[h])
+        n_to_sibling(is_away)
+
+    def pass_g(i):
+        for h in range(2):
+            arrive(g_work.at[chunk(h, i)], tg_sem.at[h, i])
+
+        @pl.when(is_away)
+        def _():
+            g_to_sibling(g_work, i, is_away)
+
+    pass_g(0)
+    pass_on(1)
+    pass_g(1)
+
+
+    @pl.when(is_away)
+    def _():
+        for h in range(2):
+            trade(lambda: q_hbm, lambda: q_work, lambda h: tq_sem.at[h], h)
 
     for j in range(2):
         arrive(n_sib.at[:, pl.ds(512 * j, 512)], sn_sem.at[j])
-    arrive(g_sib, sg_sem)
+    for i in range(2):
+        for h in range(2):
+            arrive(g_sib.at[chunk(h, i)], sg_sem.at[h, i])
     xa, xb = blocks_of(away)
 
     def product(dz):
@@ -261,54 +304,30 @@
     for k in (1, 0):
         first.append(send(lambda k=k: (d_piece(2, k, 0), r1.at[0, k], r1_sem.at[k], up)))
         first.append(send(lambda k=k: (d_piece(2, k, 1), r1.at[1, k], r1_sem.at[2 + k], down)))
+
+    for k in range(2):
+        for h in range(2):
+            arrive(w_piece(k, 2, h), w_flag(k, 2, h))
+            to_sibling(k, 2, h)
+
     product(1)
     product(3)
-    product(0)
-
-    for k in range(2):
-        for h in range(2):
-            arrive(w_piece(k, 2, h), w_flag(k, 2, h))
-            to_sibling(k, 2, h)
 
     def to_next(k, h, way):
         dz, side = (1, 0) if way == 1 else (3, 1)
         send(lambda: (d_piece(dz, k, h), r2.at[side, k, h], r2_sem.at[4 * side + 2 * k + h], up if way == 1 else down))
 
-    for n in first[:2]:
-        wait_sent(n)
-    for k in (1, 0):
+    def add_into(target, term):
+        @pl.loop(0, QKV // 512)
+        def _(j):
+            span = pl.ds(pl.multiple_of(j * 512, 512), 512)
+            target[:, span] = (target[:, span].astype(F32) + term[:, span].astype(F32)).astype(BF16)
+
+    def direct(k):
         to_next(k, 1, 1)
         to_next(k, 0, -1)
 
-    for h in range(2):
-        arrive(q_work.at[pl.ds(HALF * h, HALF)], tq_sem.at[h])
-    for dz in range(4):
-        for k in range(2):
-            for h in range(2):
-                arrive(w_piece(k, dz, h, 1), ws_flag(k, dz, h))
-
-    for block in range(4):
-
-        @pl.loop(0, 2)
-        def _(j):
-            rows = pl.ds(pl.multiple_of(512 * block + 256 * j, 256), 256)
-            out = lax.dot_general(q_work[...], w_full[rows, :], (((1,), (1,)), ((), ())), preferred_element_type=F32)
-            dirs[0, :, rows] = out.astype(BF16)
-
-        @pl.when(is_away)
-        def _():
-            columns = pl.ds(512 * block, 512)
-            for h in range(2):
-                flags = functools.partial(lambda block, i: rd_sem.at[i, block], block)
-                trade(lambda: dirs.at[0, :, columns], lambda: dirs.at[1, :, columns], flags, h)
-
-    def add_into(target, term):
-        @pl.loop(0, QKV // 512)
-        def _(j):
-            span = pl.ds(pl.multiple_of(j * 512, 512), 512)
-            target[:, span] = (target[:, span].astype(F32) + term[:, span].astype(F32)).astype(BF16)
-
-    for k in (1, 0):
+    def summed(k):
         arrive(r1.at[0, k], r1_sem.at[k])
         add_into(d_piece(1, k, 0), r1.at[0, k])
         to_next(k, 0, 1)
@@ -316,11 +335,74 @@
         add_into(d_piece(3, k, 1), r1.at[1, k])
         to_next(k, 1, -1)
 
+    for n in first[:2]:
+        wait_sent(n)
+    direct(1)
+    product(0)
+
+    def gain_copy(j, source):
+        return pltpu.make_async_remote_copy(
+            src_ref=gain_all.at[source], dst_ref=gain_all.at[source], send_sem=gsend_sem.at[j], recv_sem=gg_sem.at[source],
+            device_id=(s, (f + j) % 16), device_id_type=MESH,
+        )
+
+    for dz in range(4):
+        for k in range(2):
+            for h in range(2):
+                arrive(w_piece(k, dz, h, 1), ws_flag(k, dz, h))
+
+    @pl.loop(0, D // 256)
+    def _(j):
+        rows = pl.ds(pl.multiple_of(256 * j, 256), 256)
+        out = lax.dot_general(g_work[...], w_full[rows, :], (((1,), (1,)), ((), ())), preferred_element_type=F32)
+        gain_part[:, rows] = jnp.sum(out * normed[0, :, rows].astype(F32), axis=0, keepdims=True)
+
+    slot = 4 * (x // 2) + z
+
+    @pl.when(is_away)
+    def _():
+        send(lambda: (gain_part, gain_sib, gp_sem, sibling), is_away)
+
+    @pl.when(is_home)
+    def _():
+        arrive(gain_sib, gp_sem)
+        gain_all[slot, :, :] = gain_part[...] + gain_sib[...]
+
+        @pl.loop(1, 16)
+        def _(j):
+            gain_copy(j, slot).start()
+
+    for h in range(2):
+        arrive(q_work.at[whole(h)], tq_sem.at[h])
+
+    def direction(block):
+        @pl.loop(0, 2)
+        def _(j):
+            rows = pl.ds(pl.multiple_of(512 * block + 256 * j, 256), 256)
+            out = lax.dot_general(q_work[...], w_full[rows, :], (((1,), (1,)), ((), ())), preferred_element_type=F32)
+            dirs[0, :, rows] = out.astype(BF16)
+
+        @pl.when(is_away)
+        def _():
+            columns = pl.ds(512 * block, 512)
+            for h in range(2):
+                trade(lambda: dirs.at[0, :, columns], lambda: dirs.at[1, :, columns], lambda h: rd_sem.at[h, block], h)
+
+    direction(0)
+    direction(1)
+    for n in first[2:]:
+        wait_sent(n)
+    summed(1)
+    direct(0)
+    direction(2)
+    direction(3)
+    summed(0)
+
     @pl.when(is_away)
     def _():
         for h in range(2):
             for block in range(4):
-                arrive(dirs.at[1, pl.ds(HALF * h, HALF), pl.ds(512 * block, 512)], rd_sem.at[h, block])
+                arrive(dirs.at[1, whole(h), pl.ds(512 * block, 512)], rd_sem.at[h, block])
 
     x_load.wait()
     res_load.wait()
@@ -357,7 +439,6 @@
         sum_into(d_piece(0, 1, h), 1, h)
         send(lambda h=h: (d_piece(0, 1, h), r3.at[h], r3_sem.at[h], across))
 
-    own_load.wait()
     for h in range(2):
         r2_arrive(0, h)
         arrive(r3.at[h], r3_sem.at[h])
@@ -387,24 +468,13 @@
 
     w_store = load(wout, wg_hbm, load_sem.at[3])
 
-    def fold(i, total):
-        span = pl.ds(pl.multiple_of(i * 128, 128), 128)
-        return total + w_own[:, span].astype(F32) * wout[:, span]
-
-    folded = lax.fori_loop(0, QKV // 128, fold, jnp.zeros((OWN, 128), F32))
-    part = jnp.sum(folded.T, axis=0, keepdims=True) / gain_ref[:, pl.ds(own_rows, OWN)]
-    gain_row[...] = part
-    gg_ref[f, :, :] = part
-
-    def gain_copy(j, source):
-        return pltpu.make_async_remote_copy(
-            src_ref=gain_row, dst_ref=gg_ref.at[source], send_sem=gsend_sem.at[j], recv_sem=gg_sem.at[source],
-            device_id=(s, (f + j) % 16), device_id_type=MESH,
-        )
-
-    @pl.loop(1, 16)
-    def _(j):
-        gain_copy(j, f).start()
+    for j in range(8):
+
+        @pl.when(is_away | (slot != j))
+        def _():
+            arrive(gain_all.at[j], gg_sem.at[j])
+
+    gg_ref[...] = jnp.sum(gain_all[...], axis=0) / gain_ref[...]
 
     @pl.when(s < 7)
     def _():
@@ -412,30 +482,30 @@
             rows = pl.ds(128 * part, 128)
             arrive(up_hbm.at[rows], lg_sem.at[part])
 
-    @pl.loop(1, 16)
-    def _(j):
-        source = (f + 16 - j) % 16
-        gain_copy(j, source).wait_recv()
-        gain_copy(j, f).wait_send()
+    @pl.when(is_home)
+    def _():
+        @pl.loop(1, 16)
+        def _(j):
+            gain_copy(j, slot).wait_send()
 
     w_store.wait()
     for n in range(len(sent)):
         wait_sent(n)
 
 
-SENDS = 120
+SENDS = 128
 
 
 def local(layer_input, resid_grad, qkv_grad, prev_input, prev_qkv_grad, qkv_weight, norm_gain):
     hbm = pl.BlockSpec(memory_space=pl.ANY)
     vmem = pl.BlockSpec(memory_space=pltpu.VMEM)
     dma = pltpu.SemaphoreType.DMA
-    received, weight_grad, gain_rows = pl.pallas_call(
+    received, weight_grad, gain_grad = pl.pallas_call(
         kernel,
         out_shape=(
             jax.ShapeDtypeStruct((TOK, D), BF16),
             jax.ShapeDtypeStruct((OWN, QKV), F32),
-            jax.ShapeDtypeStruct((16, 1, OWN), F32),
+            jax.ShapeDtypeStruct((1, D), F32),
         ),
         in_specs=[hbm] * 6 + [vmem],
         out_specs=(hbm, hbm, vmem),
@@ -447,7 +517,6 @@
             pltpu.VMEM((2, PIECE, QKV), BF16),
             pltpu.VMEM((2, PIECE, QKV), BF16),
             pltpu.VMEM((OWN, QKV), F32),
-            pltpu.VMEM((OWN, QKV), BF16),
             pltpu.VMEM((TOK, QKV), BF16),
             pltpu.VMEM((2, TOK, D), BF16),
             pltpu.VMEM((TOK, D // 2), BF16),
@@ -456,22 +525,25 @@
             pltpu.VMEM((2, TOK, D), BF16),
             pltpu.VMEM((TOK, D), BF16),
             pltpu.VMEM((TOK, D), BF16),
-            pltpu.VMEM((1, OWN), F32),
+            pltpu.VMEM((1, D), F32),
+            pltpu.VMEM((1, D), F32),
+            pltpu.VMEM((8, 1, D), F32),
             dma((4,)),
             dma((32,)),
             dma((32,)),
             dma((2,)),
+            dma((2, 2)),
             dma((2,)),
             dma((2,)),
-            dma((2,)),
-            dma(()),
+            dma((2, 2)),
             dma((2, 4)),
             dma((4,)),
             dma((8,)),
             dma((2,)),
             dma((2,)),
             dma((4,)),
-            dma((16,)),
+            dma(()),
+            dma((8,)),
             dma((SENDS,)),
             dma((16,)),
         ],
@@ -479,7 +551,7 @@
     )(layer_input[0], resid_grad[0], qkv_grad[0], prev_input[0], prev_qkv_grad[0], qkv_weight[0], norm_gain)
     last = lax.axis_index("section") == lax.axis_size("section") - 1
     upstream_grad = jnp.where(last, jnp.zeros_like(received), received)
-    return (upstream_grad[None], weight_grad[None], gain_rows.reshape(1, D))
+    return (upstream_grad[None], weight_grad[None], gain_grad)
 
 
 def solution(mesh):

time: 153 us -> 140 us (0.915); the launches traced: 151 us -> 140 us
  Pallas kernels: 145 us -> 135 us
    pallas_call x1, Pallas kernels: 145 us -> 135 us  [local(): pl.pallas_call(kernel, out_shape=(jax.ShapeDtypeStruct((TOK, D), BF16), j...]
where the time goes in v3:
time: 140 us
  Pallas kernels  135 us (96%)
  other arithmetic  3.17 us (2%)
  local copies, waits for them, and re-layouts  1.75 us (1%)
    pallas_call x1, Pallas kernels, local(): pl.pallas_call(kernel, out_shape=(jax.ShapeDtypeStruct((TOK, D), BF16), j...  135 us
    broadcast_in_dim x1, other arithmetic, local(): return (upstream_grad[None], weight_grad[None], gain_grad)  3.17 us

profile of v3, /device:TPU:1, one launch (start us, length us, event | category | flops | bytes accessed | tf_op | source)
XLA Modules:
  0.0 140.1 jit_solution(7296764002854483806)
XLA Ops:
  0.6 134.5 %shard_map.94 = (bf16[512,2048]{1,0:T(8,128)(2,1)}, f32[128,3072]{1,0:T(8,128)}, f32[1,2048]{1,0:T(1,128)}) custom-call(bf16[512,2048]{1,0:T(8,128)(2,1)} %bitcast.11, bf16[512,2048]{1,0:T(8,128)(2,1)} %bitcast.12, bf16[512,3072]{1,0:T(8,128)(2,1)} %bitcast.9, bf16[512,2048]{1,0:T(8,128)(2,1)} %bitcast.13, bf16[512,3072]{1,0:T(8,128)(2,1)} %bitcast.10, ...), custom_call_target="tpu_custom_call" | custom-call | tf_op jit(solution)/shard_map/pallas_call | solution.py:503
  135.1 0.0 copy-start
  135.2 3.2 %select_bitcast_fusion = bf16[1,512,2048]{2,1,0:T(8,128)(2,1)} fusion(bf16[512,2048]{1,0:T(8,128)(2,1)} %get-tuple-element.6, pred[]{:T(512)S(6)} %eq.3), kind=kLoop, calls=%fused_computation | loop fusion | flops 1048576 | bytes 4194305 | tf_op jit(solution)/shard_map/broadcast_in_dim | solution.py:554
  138.3 0.0 copy-start.1
  138.3 0.0 copy-done
  138.3 1.1 copy.12
  139.5 0.0 copy-done.1
  139.5 0.6 copy.13
Async XLA Ops:
  135.1 3.2 %copy-start = (f32[128,3072]{1,0:T(8,128)S(1)}, f32[128,3072]{1,0:T(8,128)}, u32[]{:S(2)}) copy-start(f32[128,3072]{1,0:T(8,128)} %get-tuple-element.7) | copy-start | bytes 4718596
  138.3 1.1 copy-start.1

commit v4 on v3

--- a/solution.py
+++ b/solution.py
@@ -114,11 +114,11 @@
     def ws_flag(k, dz, h):
         return ws_sem.at[8 * ((dz + 4) % 4) + 2 * k + h]
 
-    def to_sibling(k, dz, h):
-        send(lambda: (w_piece(k, dz, h), w_piece(k, dz, h), ws_flag(k, dz, h), sibling))
-
-    def to_z(k, dz, h, way):
-        send(lambda: (w_piece(k, dz, h), w_piece(k, dz, h), w_flag(k, dz - way, h), up if way == 1 else down))
+    def to_sibling(k, dz, h, when=None):
+        send(lambda: (w_piece(k, dz, h), w_piece(k, dz, h), ws_flag(k, dz, h), sibling), when)
+
+    def to_z(k, dz, h, way, when=None):
+        send(lambda: (w_piece(k, dz, h), w_piece(k, dz, h), w_flag(k, dz - way, h), up if way == 1 else down), when)
 
     def own_across(source, when):
         for h in range(2):
@@ -144,13 +144,14 @@
 
     @pl.when(is_away)
     def _():
-        for h in range(2):
-
-            def own_piece(h=h):
-                rows = w_full.at[pl.ds(pl.multiple_of(own_rows + PIECE * h, PIECE), PIECE)]
-                return half_rows(h), rows, w_flag(0, 0, 1 - h), right if h == 1 else left
-
-            send(own_piece, is_away)
+        for k in range(2):
+            for h in range(2):
+
+                def own_piece(k=k, h=h):
+                    rows = w_full.at[pl.ds(pl.multiple_of(own_rows + PIECE * h, PIECE), PIECE)]
+                    return half_rows(h), rows, w_flag(k, 0, 1 - h), right if h != k else left
+
+                send(own_piece, is_away)
 
     prev_load = load(prev_hbm, x_buf, load_sem.at[0])
     res_load = load(res_hbm, res_buf, load_sem.at[2])
@@ -208,7 +209,6 @@
 
     @pl.when(is_away)
     def _():
-        own_across(lambda h: w_piece(0, 0, h), is_away)
         spread_own(lambda h: w_piece(0, 0, h), is_away)
         for h in range(2):
             trade(lambda: normed.at[1], lambda: normed.at[0], lambda h: tn_sem.at[h], h)
@@ -221,6 +221,22 @@
             g_to_sibling(g_hbm, i, is_home)
 
     x_load = load(x_hbm, x_buf, load_sem.at[0])
+
+    def pass_on(k, when=None):
+        for h in range(2):
+            arrive(w_piece(k, -1, h), w_flag(k, -1, h))
+            if h == 0:
+                to_z(k, -1, 0, 1, when)
+            arrive(w_piece(k, 1, h), w_flag(k, 1, h))
+            if h == 1:
+                to_z(k, 1, 1, -1, when)
+        for h in range(2):
+            to_sibling(k, -1, h, when)
+            to_sibling(k, 1, h, when)
+
+    @pl.when(is_home)
+    def _():
+        pass_on(0, is_home)
 
     for h in range(2):
         arrive(w_piece(1, 0, h), w_flag(1, 0, h))
@@ -231,19 +247,7 @@
     @pl.when(is_away)
     def _():
         trade_g(0)
-
-    def pass_on(k):
-        for h in range(2):
-            arrive(w_piece(k, -1, h), w_flag(k, -1, h))
-            if h == 0:
-                to_z(k, -1, 0, 1)
-            arrive(w_piece(k, 1, h), w_flag(k, 1, h))
-            if h == 1:
-                to_z(k, 1, 1, -1)
-            to_sibling(k, -1, h)
-            to_sibling(k, 1, h)
-
-    pass_on(0)
+        pass_on(0, is_away)
 
     @pl.when(is_away)
     def _():
@@ -300,10 +304,14 @@
         return dw.at[dz, pl.ds(pl.multiple_of(at_home + away * (at_away - at_home), PIECE), PIECE)]
 
     product(2)
-    first = []
-    for k in (1, 0):
-        first.append(send(lambda k=k: (d_piece(2, k, 0), r1.at[0, k], r1_sem.at[k], up)))
-        first.append(send(lambda k=k: (d_piece(2, k, 1), r1.at[1, k], r1_sem.at[2 + k], down)))
+
+    def farthest(k):
+        return [
+            send(lambda: (d_piece(2, k, 0), r1.at[0, k], r1_sem.at[k], up)),
+            send(lambda: (d_piece(2, k, 1), r1.at[1, k], r1_sem.at[2 + k], down)),
+        ]
+
+    first, second = farthest(1), farthest(0)
 
     for k in range(2):
         for h in range(2):
@@ -335,7 +343,7 @@
         add_into(d_piece(3, k, 1), r1.at[1, k])
         to_next(k, 1, -1)
 
-    for n in first[:2]:
+    for n in first:
         wait_sent(n)
     direct(1)
     product(0)
@@ -351,11 +359,14 @@
             for h in range(2):
                 arrive(w_piece(k, dz, h, 1), ws_flag(k, dz, h))
 
-    @pl.loop(0, D // 256)
-    def _(j):
-        rows = pl.ds(pl.multiple_of(256 * j, 256), 256)
-        out = lax.dot_general(g_work[...], w_full[rows, :], (((1,), (1,)), ((), ())), preferred_element_type=F32)
-        gain_part[:, rows] = jnp.sum(out * normed[0, :, rows].astype(F32), axis=0, keepdims=True)
+    def gain_blocks(start, stop):
+        @pl.loop(start, stop)
+        def _(j):
+            rows = pl.ds(pl.multiple_of(256 * j, 256), 256)
+            out = lax.dot_general(g_work[...], w_full[rows, :], (((1,), (1,)), ((), ())), preferred_element_type=F32)
+            gain_part[:, rows] = jnp.sum(out * normed[0, :, rows].astype(F32), axis=0, keepdims=True)
+
+    gain_blocks(0, 8)
 
     slot = 4 * (x // 2) + z
 
@@ -390,7 +401,7 @@
 
     direction(0)
     direction(1)
-    for n in first[2:]:
+    for n in second:
         wait_sent(n)
     summed(1)
     direct(0)
@@ -434,37 +445,50 @@
         arrive(r2.at[0, k, h], r2_sem.at[2 * k + h])
         arrive(r2.at[1, k, h], r2_sem.at[4 + 2 * k + h])
 
+    def to_owner(k, h):
+        send(lambda: (d_piece(0, k, h), r4.at[k, 1 - h], r4_sem.at[k, 1 - h], left if h == k else right), is_away)
+
     for h in range(2):
         r2_arrive(1, h)
         sum_into(d_piece(0, 1, h), 1, h)
-        send(lambda h=h: (d_piece(0, 1, h), r3.at[h], r3_sem.at[h], across))
+
+        @pl.when(is_home)
+        def _():
+            send(lambda h=h: (d_piece(0, 1, h), r3.at[h], r3_sem.at[h], across), is_home)
+
+        @pl.when(is_away)
+        def _():
+            to_owner(1, h)
 
     for h in range(2):
         r2_arrive(0, h)
-        arrive(r3.at[h], r3_sem.at[h])
-        target = d_piece(0, 0, h)
-
-        @pl.loop(0, QKV // 512)
-        def _(j):
-            span = pl.ds(pl.multiple_of(j * 512, 512), 512)
-            total = target[:, span].astype(F32) + r2[0, 0, h, :, span].astype(F32) + r2[1, 0, h, :, span].astype(F32)
-            total += r3[h, :, span].astype(F32)
-            wout[pl.ds(PIECE * h, PIECE), span] = total
-            target[:, span] = total.astype(BF16)
 
         @pl.when(is_away)
         def _():
-            send(lambda h=h: (d_piece(0, 0, h), r4.at[1 - h], r4_sem.at[1 - h], left if h == 0 else right), is_away)
-
-    @pl.when(is_away)
-    def _():
-        for h in range(2):
-            arrive(r4.at[h], r4_sem.at[h])
+            sum_into(d_piece(0, 0, h), 0, h)
+            to_owner(0, h)
+
+        @pl.when(is_home)
+        def _():
+            arrive(r3.at[h], r3_sem.at[h])
+            target = d_piece(0, 0, h)
 
             @pl.loop(0, QKV // 512)
             def _(j):
                 span = pl.ds(pl.multiple_of(j * 512, 512), 512)
-                wout[pl.ds(PIECE * h, PIECE), span] = r4[h, :, span].astype(F32)
+                total = target[:, span].astype(F32) + r2[0, 0, h, :, span].astype(F32) + r2[1, 0, h, :, span].astype(F32)
+                wout[pl.ds(PIECE * h, PIECE), span] = total + r3[h, :, span].astype(F32)
+
+    @pl.when(is_away)
+    def _():
+        for h in range(2):
+            for k in range(2):
+                arrive(r4.at[k, h], r4_sem.at[k, h])
+
+            @pl.loop(0, QKV // 512)
+            def _(j):
+                span = pl.ds(pl.multiple_of(j * 512, 512), 512)
+                wout[pl.ds(PIECE * h, PIECE), span] = r4[0, h, :, span].astype(F32) + r4[1, h, :, span].astype(F32)
 
     w_store = load(wout, wg_hbm, load_sem.at[3])
 
@@ -493,7 +517,7 @@
         wait_sent(n)
 
 
-SENDS = 128
+SENDS = 140
 
 
 def local(layer_input, resid_grad, qkv_grad, prev_input, prev_qkv_grad, qkv_weight, norm_gain):
@@ -515,7 +539,7 @@
             pltpu.VMEM((2, 2, PIECE, QKV), BF16),
             pltpu.VMEM((2, 2, 2, PIECE, QKV), BF16),
             pltpu.VMEM((2, PIECE, QKV), BF16),
-            pltpu.VMEM((2, PIECE, QKV), BF16),
+            pltpu.VMEM((2, 2, PIECE, QKV), BF16),
             pltpu.VMEM((OWN, QKV), F32),
             pltpu.VMEM((TOK, QKV), BF16),
             pltpu.VMEM((2, TOK, D), BF16),
@@ -540,7 +564,7 @@
             dma((4,)),
             dma((8,)),
             dma((2,)),
-            dma((2,)),
+            dma((2, 2)),
             dma((4,)),
             dma(()),
             dma((8,)),

time: 140 us -> 128 us (0.914)
  Pallas kernels: 135 us -> 122 us
    pallas_call x1, Pallas kernels: 135 us -> 122 us  [local(): pl.pallas_call(kernel, out_shape=(jax.ShapeDtypeStruct((TOK, D), BF16), j...]
where the time goes in v4:
time: 128 us
  Pallas kernels  122 us (95%)
  other arithmetic  3.17 us (2%)
  local copies, waits for them, and re-layouts  1.75 us (1%)
    pallas_call x1, Pallas kernels, local(): pl.pallas_call(kernel, out_shape=(jax.ShapeDtypeStruct((TOK, D), BF16), j...  122 us
    broadcast_in_dim x1, other arithmetic, local(): return (upstream_grad[None], weight_grad[None], gain_grad)  3.17 us

profile of v4, /device:TPU:1, one launch (start us, length us, event | category | flops | bytes accessed | tf_op | source)
XLA Modules:
  0.0 127.7 jit_solution(10657425421010651348)
XLA Ops:
  0.6 122.1 %shard_map.94 = (bf16[512,2048]{1,0:T(8,128)(2,1)}, f32[128,3072]{1,0:T(8,128)}, f32[1,2048]{1,0:T(1,128)}) custom-call(bf16[512,2048]{1,0:T(8,128)(2,1)} %bitcast.11, bf16[512,2048]{1,0:T(8,128)(2,1)} %bitcast.12, bf16[512,3072]{1,0:T(8,128)(2,1)} %bitcast.9, bf16[512,2048]{1,0:T(8,128)(2,1)} %bitcast.13, bf16[512,3072]{1,0:T(8,128)(2,1)} %bitcast.10, ...), custom_call_target="tpu_custom_call" | custom-call | tf_op jit(solution)/shard_map/pallas_call | solution.py:527
  122.7 0.0 copy-start
  122.7 3.2 %select_bitcast_fusion = bf16[1,512,2048]{2,1,0:T(8,128)(2,1)} fusion(bf16[512,2048]{1,0:T(8,128)(2,1)} %get-tuple-element.6, pred[]{:T(512)S(6)} %eq.3), kind=kLoop, calls=%fused_computation | loop fusion | flops 1048576 | bytes 4194305 | tf_op jit(solution)/shard_map/broadcast_in_dim | solution.py:578
  125.9 0.0 copy-start.1
  125.9 0.0 copy-done
  125.9 1.1 copy.12
  127.1 0.0 copy-done.1
  127.1 0.6 copy.13
Async XLA Ops:
  122.7 3.2 %copy-start = (f32[128,3072]{1,0:T(8,128)S(1)}, f32[128,3072]{1,0:T(8,128)}, u32[]{:S(2)}) copy-start(f32[128,3072]{1,0:T(8,128)} %get-tuple-element.7) | copy-start | bytes 4718596
  125.9 1.1 copy-start.1

commit v5 on v4

--- a/solution.py
+++ b/solution.py
@@ -343,17 +343,7 @@
         add_into(d_piece(3, k, 1), r1.at[1, k])
         to_next(k, 1, -1)
 
-    for n in first:
-        wait_sent(n)
-    direct(1)
     product(0)
-
-    def gain_copy(j, source):
-        return pltpu.make_async_remote_copy(
-            src_ref=gain_all.at[source], dst_ref=gain_all.at[source], send_sem=gsend_sem.at[j], recv_sem=gg_sem.at[source],
-            device_id=(s, (f + j) % 16), device_id_type=MESH,
-        )
-
     for dz in range(4):
         for k in range(2):
             for h in range(2):
@@ -366,22 +356,18 @@
             out = lax.dot_general(g_work[...], w_full[rows, :], (((1,), (1,)), ((), ())), preferred_element_type=F32)
             gain_part[:, rows] = jnp.sum(out * normed[0, :, rows].astype(F32), axis=0, keepdims=True)
 
-    gain_blocks(0, 8)
-
-    slot = 4 * (x // 2) + z
-
-    @pl.when(is_away)
-    def _():
-        send(lambda: (gain_part, gain_sib, gp_sem, sibling), is_away)
-
-    @pl.when(is_home)
-    def _():
-        arrive(gain_sib, gp_sem)
-        gain_all[slot, :, :] = gain_part[...] + gain_sib[...]
-
-        @pl.loop(1, 16)
-        def _(j):
-            gain_copy(j, slot).start()
+    gain_blocks(0, 4)
+
+    for n in first:
+        wait_sent(n)
+    direct(1)
+
+    def gain_copy(j, source):
+        return pltpu.make_async_remote_copy(
+            src_ref=gain_all.at[source], dst_ref=gain_all.at[source], send_sem=gsend_sem.at[j], recv_sem=gg_sem.at[source],
+            device_id=(s, (f + j) % 16), device_id_type=MESH,
+        )
+
 
     for h in range(2):
         arrive(q_work.at[whole(h)], tq_sem.at[h])
@@ -408,6 +394,7 @@
     direction(2)
     direction(3)
     summed(0)
+    gain_blocks(4, 8)
 
     @pl.when(is_away)
     def _():
@@ -434,6 +421,21 @@
             rows = pl.ds(128 * part, 128)
             send(lambda part=part: (res_buf.at[rows], up_hbm.at[rows], lg_sem.at[part], before), has_before)
 
+    slot = 4 * (x // 2) + z
+
+    @pl.when(is_away)
+    def _():
+        send(lambda: (gain_part, gain_sib, gp_sem, sibling), is_away)
+
+    @pl.when(is_home)
+    def _():
+        arrive(gain_sib, gp_sem)
+        gain_all[slot, :, :] = gain_part[...] + gain_sib[...]
+
+        @pl.loop(1, 16)
+        def _(j):
+            gain_copy(j, slot).start()
+
     def sum_into(target, k, h):
         @pl.loop(0, QKV // 512)
         def _(j):
@@ -518,6 +520,28 @@
 
 
 SENDS = 140
+
+
+def place(received, weight, gain, up_out, weight_out, gain_out, up_buf, weight_buf, gain_buf, in_sem, out_sem):
+    last = lax.axis_index("section") == 7
+    parts = [(received, up_buf, up_out, pl.ds(128 * i, 128)) for i in range(4)]
+    parts += [(weight, weight_buf, weight_out, pl.ds(32 * i, 32)) for i in range(4)]
+    parts.append((gain, gain_buf, gain_out, pl.ds(0, 1)))
+    reads = [pltpu.make_async_copy(src.at[rows], buf.at[rows], in_sem.at[i]) for i, (src, buf, _, rows) in enumerate(parts)]
+    writes = [pltpu.make_async_copy(buf.at[rows], dst.at[rows], out_sem.at[i]) for i, (_, buf, dst, rows) in enumerate(parts)]
+    for read in reads:
+        read.start()
+    for i in range(9):
+        reads[i].wait()
+        if i < 4:
+
+            @pl.when(last)
+            def _():
+                up_buf[parts[i][3], :] = jnp.zeros((128, D), BF16)
+
+        writes[i].start()
+    for write in writes:
+        write.wait()
 
 
 def local(layer_input, resid_grad, qkv_grad, prev_input, prev_qkv_grad, qkv_weight, norm_gain):
@@ -573,8 +597,17 @@
         ],
         compiler_params=pltpu.CompilerParams(collective_id=0, has_side_effects=True, vmem_limit_bytes=62 << 20),
     )(layer_input[0], resid_grad[0], qkv_grad[0], prev_input[0], prev_qkv_grad[0], qkv_weight[0], norm_gain)
-    last = lax.axis_index("section") == lax.axis_size("section") - 1
-    upstream_grad = jnp.where(last, jnp.zeros_like(received), received)
+    upstream_grad, weight_grad, gain_grad = pl.pallas_call(
+        place,
+        out_shape=(
+            jax.ShapeDtypeStruct((TOK, D), BF16),
+            jax.ShapeDtypeStruct((OWN, QKV), F32),
+            jax.ShapeDtypeStruct((1, D), F32),
+        ),
+        in_specs=[hbm] * 3,
+        out_specs=(hbm, hbm, hbm),
+        scratch_shapes=[pltpu.VMEM((TOK, D), BF16), pltpu.VMEM((OWN, QKV), F32), pltpu.VMEM((1, D), F32), dma((9,)), dma((9,))],
+    )(received, weight_grad, gain_grad)
     return (upstream_grad[None], weight_grad[None], gain_grad)
 
 

time: 128 us -> 126 us (0.984)
  other arithmetic: 3.17 us -> 0 us
  Pallas kernels: 122 us -> 125 us
  local copies, waits for them, and re-layouts: 1.75 us -> 0 us
    broadcast_in_dim x1 -> x0, other arithmetic: 3.17 us -> none  [local(): return (upstream_grad[None], weight_grad[None], gain_grad)]
    pallas_call x0 -> x1, Pallas kernels: none -> 3.03 us  [local(): pl.pallas_call(place, out_shape=(jax.ShapeDtypeStruct((TOK, D), BF16), ja...]
    unnamed x6 -> x0, local copies, waits for them, and re-layouts: 1.75 us -> none
where the time goes in v5:
time: 126 us
  Pallas kernels  125 us (99%)
    pallas_call x1, Pallas kernels, local(): pl.pallas_call(kernel, out_shape=(jax.ShapeDtypeStruct((TOK, D), BF16), j...  122 us
    pallas_call x1, Pallas kernels, local(): pl.pallas_call(place, out_shape=(jax.ShapeDtypeStruct((TOK, D), BF16), ja...  3.03 us

profile of v5, /device:TPU:1, one launch (start us, length us, event | category | flops | bytes accessed | tf_op | source)
XLA Modules:
  0.0 125.7 jit_solution(14579089687056996234)
XLA Ops:
  0.6 122.1 %shard_map.94 = (bf16[512,2048]{1,0:T(8,128)(2,1)}, f32[128,3072]{1,0:T(8,128)}, f32[1,2048]{1,0:T(1,128)}) custom-call(bf16[512,2048]{1,0:T(8,128)(2,1)} %bitcast.10, bf16[512,2048]{1,0:T(8,128)(2,1)} %bitcast.11, bf16[512,3072]{1,0:T(8,128)(2,1)} %bitcast.8, bf16[512,2048]{1,0:T(8,128)(2,1)} %bitcast.12, bf16[512,3072]{1,0:T(8,128)(2,1)} %bitcast.9, ...), custom_call_target="tpu_custom_call" | custom-call | tf_op jit(solution)/shard_map/pallas_call | solution.py:551
  122.7 3.0 %shard_map.95 = (bf16[512,2048]{1,0:T(8,128)(2,1)}, f32[128,3072]{1,0:T(8,128)}, f32[1,2048]{1,0:T(1,128)}) custom-call(bf16[512,2048]{1,0:T(8,128)(2,1)} %get-tuple-element.9.received, f32[128,3072]{1,0:T(8,128)} %get-tuple-element.10.weight, f32[1,2048]{1,0:T(1,128)} %get-tuple-element.11.gain), custom_call_target="tpu_custom_call" | custom-call | tf_op jit(solution)/shard_map/pallas_call | solution.py:600

commit v6 on v5

--- a/solution.py
+++ b/solution.py
@@ -212,6 +212,7 @@
         spread_own(lambda h: w_piece(0, 0, h), is_away)
         for h in range(2):
             trade(lambda: normed.at[1], lambda: normed.at[0], lambda h: tn_sem.at[h], h)
+        trade_g(0)
 
     @pl.when(is_home)
     def _():
@@ -246,7 +247,6 @@
 
     @pl.when(is_away)
     def _():
-        trade_g(0)
         pass_on(0, is_away)
 
     @pl.when(is_away)
@@ -358,8 +358,6 @@
 
     gain_blocks(0, 4)
 
-    for n in first:
-        wait_sent(n)
     direct(1)
 
     def gain_copy(j, source):
@@ -394,7 +392,6 @@
     direction(2)
     direction(3)
     summed(0)
-    gain_blocks(4, 8)
 
     @pl.when(is_away)
     def _():
@@ -421,21 +418,6 @@
             rows = pl.ds(128 * part, 128)
             send(lambda part=part: (res_buf.at[rows], up_hbm.at[rows], lg_sem.at[part], before), has_before)
 
-    slot = 4 * (x // 2) + z
-
-    @pl.when(is_away)
-    def _():
-        send(lambda: (gain_part, gain_sib, gp_sem, sibling), is_away)
-
-    @pl.when(is_home)
-    def _():
-        arrive(gain_sib, gp_sem)
-        gain_all[slot, :, :] = gain_part[...] + gain_sib[...]
-
-        @pl.loop(1, 16)
-        def _(j):
-            gain_copy(j, slot).start()
-
     def sum_into(target, k, h):
         @pl.loop(0, QKV // 512)
         def _(j):
@@ -461,6 +443,23 @@
         @pl.when(is_away)
         def _():
             to_owner(1, h)
+
+    gain_blocks(4, 8)
+
+    slot = 4 * (x // 2) + z
+
+    @pl.when(is_away)
+    def _():
+        send(lambda: (gain_part, gain_sib, gp_sem, sibling), is_away)
+
+    @pl.when(is_home)
+    def _():
+        arrive(gain_sib, gp_sem)
+        gain_all[slot, :, :] = gain_part[...] + gain_sib[...]
+
+        @pl.loop(1, 16)
+        def _(j):
+            gain_copy(j, slot).start()
 
     for h in range(2):
         r2_arrive(0, h)

time: 126 us -> 126 us (level)
  no operation moved by 1% of the time
where the time goes in v6:
time: 126 us; the launch traced here: 125 us
  Pallas kernels  125 us (99%)
    pallas_call x1, Pallas kernels, local(): pl.pallas_call(kernel, out_shape=(jax.ShapeDtypeStruct((TOK, D), BF16), j...  122 us
    pallas_call x1, Pallas kernels, local(): pl.pallas_call(place, out_shape=(jax.ShapeDtypeStruct((TOK, D), BF16), ja...  3.03 us

profile of v6, /device:TPU:1, one launch (start us, length us, event | category | flops | bytes accessed | tf_op | source)
XLA Modules:
  0.0 125.3 jit_solution(10903661427790865889)
XLA Ops:
  0.6 121.7 %shard_map.94 = (bf16[512,2048]{1,0:T(8,128)(2,1)}, f32[128,3072]{1,0:T(8,128)}, f32[1,2048]{1,0:T(1,128)}) custom-call(bf16[512,2048]{1,0:T(8,128)(2,1)} %bitcast.10, bf16[512,2048]{1,0:T(8,128)(2,1)} %bitcast.11, bf16[512,3072]{1,0:T(8,128)(2,1)} %bitcast.8, bf16[512,2048]{1,0:T(8,128)(2,1)} %bitcast.12, bf16[512,3072]{1,0:T(8,128)(2,1)} %bitcast.9, ...), custom_call_target="tpu_custom_call" | custom-call | tf_op jit(solution)/shard_map/pallas_call | solution.py:550
  122.3 3.0 %shard_map.95 = (bf16[512,2048]{1,0:T(8,128)(2,1)}, f32[128,3072]{1,0:T(8,128)}, f32[1,2048]{1,0:T(1,128)}) custom-call(bf16[512,2048]{1,0:T(8,128)(2,1)} %get-tuple-element.9.received, f32[128,3072]{1,0:T(8,128)} %get-tuple-element.10.weight, f32[1,2048]{1,0:T(1,128)} %get-tuple-element.11.gain), custom_call_target="tpu_custom_call" | custom-call | tf_op jit(solution)/shard_map/pallas_call | solution.py:599
